TPU v7x, 128 devices: a whole 4x4x4 slice. The times are simulated.
128 devices in a mesh: gx: 32 (over z, x, core), gy: 4 (over y).
Axes of the slice: x: 4, y: 4, z: 4, core: 2. Of those that a mesh axis runs over, the one named last changes fastest.
Arguments:
- leaf_maps: float32 [1, 4096, 32768], P(None, 'gy', 'gx'), may hold values from -5 to 14, as said below
Outputs:
- quad_maps: float32 [1, 4096, 32768], P(None, 'gy', 'gx')
Inputs may be any that keep to these rules, and one draw needn't show every extreme that they name: `leaf_maps`: every patch's block is symmetric and positive definite.
All inputs are finite; a program needn't handle non-finite values.
Results may differ from a plain program's by a relative error of at most 0.000067.
Values sent between devices are 32-bit elements; how exact they have to be, the bound alone decides.
A program may use at most 128 MiB of HBM per device.

v0:
```python
import jax
import jax.numpy as jnp
from jax import lax
from jax.sharding import PartitionSpec as P


def partner_2(value, axis, apart):
    mask = 2**apart
    pairs = [(source, source ^ mask) for source in range(lax.axis_size(axis))]
    return lax.ppermute(value, axis, pairs)


def pick_rows(matrix, labels, row_labels, edge_width):
    return jnp.concatenate(
        [
            matrix[
                :,
                labels.index(label_id) * edge_width : (labels.index(label_id) + 1) * edge_width,
                :,
            ]
            for label_id in row_labels
        ],
        axis=1,
    )


def pick_cols(matrix, labels, col_labels, edge_width):
    return jnp.concatenate(
        [
            matrix[
                :,
                :,
                labels.index(label_id) * edge_width : (labels.index(label_id) + 1) * edge_width,
            ]
            for label_id in col_labels
        ],
        axis=2,
    )


def cholesky_apply(coupling, target):
    factor = jnp.linalg.cholesky(coupling)
    half_way = jax.scipy.linalg.solve_triangular(factor, target, lower=True)
    return jax.scipy.linalg.solve_triangular(factor, half_way, lower=True, trans=1)


def merge(first_map, first_labels, second_map, second_labels, shared, out_order, edge_width):
    coupling = pick_cols(
        pick_rows(first_map, first_labels, shared, edge_width), first_labels, shared, edge_width
    )
    coupling = coupling + pick_cols(
        pick_rows(second_map, second_labels, shared, edge_width), second_labels, shared, edge_width
    )
    pieces = []
    direct_rows = []
    for label_id in out_order:
        if label_id in first_labels:
            source, source_labels = (first_map, first_labels)
        else:
            source, source_labels = (second_map, second_labels)
        row_band = pick_rows(source, source_labels, [label_id], edge_width)
        pieces.append(pick_cols(row_band, source_labels, shared, edge_width))
        blocks = []
        for other_id in out_order:
            if other_id in source_labels:
                blocks.append(pick_cols(row_band, source_labels, [other_id], edge_width))
            else:
                blocks.append(jnp.zeros((row_band.shape[0], edge_width, edge_width), jnp.float32))
        direct_rows.append(jnp.concatenate(blocks, axis=2))
    edge_rows = jnp.concatenate(pieces, axis=1)
    direct = jnp.concatenate(direct_rows, axis=1)
    solved = cholesky_apply(coupling, jnp.swapaxes(edge_rows, 1, 2))
    return direct - jnp.einsum("fik,fkj->fij", edge_rows, solved, precision=lax.Precision.HIGHEST)


def body(leaf_maps):
    edge_width = leaf_maps.shape[1] // 4
    block_span = 4 * edge_width
    column_bit = lax.axis_index("gx") // (lax.axis_size("gx") // 2)
    row_bit = lax.axis_index("gy") // (lax.axis_size("gy") // 2)
    far_x = lax.axis_size("gx").bit_length() - 2
    far_y = lax.axis_size("gy").bit_length() - 2
    partner = partner_2(leaf_maps, "gy", far_y)
    lower_leaf = jnp.where(row_bit == 0, leaf_maps, partner)
    upper_leaf = jnp.where(row_bit == 0, partner, leaf_maps)
    column_map = merge(
        lower_leaf, [0, 1, 2, 9], upper_leaf, [3, 4, 9, 5], [9], [0, 3, 1, 4, 2, 5], edge_width
    )
    beside = partner_2(column_map, "gx", far_x)
    left_map = jnp.where(column_bit == 0, column_map, beside)
    right_map = jnp.where(column_bit == 0, beside, column_map)
    whole_quad = merge(
        left_map,
        [0, 1, 8, 9, 4, 6],
        right_map,
        [8, 9, 2, 3, 5, 7],
        [8, 9],
        [0, 2, 4, 5, 1, 3, 6, 7],
        edge_width,
    )
    row_band = lax.dynamic_slice_in_dim(whole_quad, row_bit * block_span, block_span, 1)
    return lax.dynamic_slice_in_dim(row_band, column_bit * block_span, block_span, 2)


def solution(mesh):
    return jax.shard_map(
        body,
        mesh=mesh,
        in_specs=(P(None, "gy", "gx"),),
        out_specs=P(None, "gy", "gx"),
        check_vma=False,
    )
```

profile of v0, /device:TPU:0, one launch (start us, length us, event | category | flops | bytes accessed | tf_op | source)
XLA Modules:
  0.0 677.4 jit_solution(4379635162620045028)
XLA Ops:
  0.0 5.3 copy.16
  5.3 3.3 collective-permute-start
  8.7 90.8 %collective-permute-done = f32[1,1024,1024]{1,2,0:T(8,128)} collective-permute-done((f32[1,1024,1024]{1,2,0:T(8,128)}, f32[1,1024,1024]{1,2,0:T(8,128)}, u32[]{:S(2)}, u32[]{:S(2)}) %collective-permute-start) | collective-permute-done | bytes 4194336 | tf_op jit(solution)/shard_map/ppermute | solution.py:10
  99.5 4.4 broadcast_select_fusion.2
  114.7 11.7 %custom-call.51 = f32[1,128,128]{2,1,0:T(8,128)S(1)} custom-call(f32[1,128,128]{2,1,0:T(8,128)S(1)} %copy.19), custom_call_target="Cholesky" | custom-call | tf_op jit(solution)/shard_map/jit(cholesky)/cholesky | solution.py:42
  126.5 9.8 %custom-call.62 = f32[1,1,128,128]{2,3,1,0:T(8,128)S(1)} custom-call(f32[1,1,128,128]{3,2,1,0:T(8,128)S(1)} %get-tuple-element.121), custom_call_target="InvertDiagBlocksLowerTriangular" | custom-call | tf_op jit(solution)/shard_map/jit(cholesky)/cholesky/custom-call.10 | solution.py:42
  139.4 12.5 %custom-call.52 = f32[1,128,128]{2,1,0:T(8,128)S(1)} custom-call(f32[1,128,128]{2,1,0:T(8,128)} %copy.21), custom_call_target="Cholesky" | custom-call | tf_op jit(solution)/shard_map/jit(cholesky)/cholesky | solution.py:42
  156.6 7.7 %while.2 = (s32[]{:T(128)}, f32[256,256]{0,1:T(8,128)}, s32[2,2]{1,0:T(2,128)S(1)}, f32[2,128,128]{2,1,0:T(8,128)}, s32[]{:T(128)}) while((s32[]{:T(128)}, f32[256,256]{0,1:T(8,128)}, s32[2,2]{1,0:T(2,128)S(1)}, f32[2,128,128]{2,1,0:T(8,128)}, s32[]{:T(128)}) %tuple.94), condition=%wide.while_cond, body=%wide.while_body.sunk | while | flops 2 | bytes 393329 | solution.py:44
  157.6 2.3 dynamic-slice.22
  161.3 2.2 dynamic-slice.22
  164.3 20.5 %custom-call.53 = f32[2,128,128]{1,2,0:T(8,128)S(1)} custom-call(f32[2,128,128]{2,1,0:T(8,128)} %get-tuple-element.13), custom_call_target="InvertDiagBlocksLowerTriangular" | custom-call | tf_op jit(solution)/shard_map/jit(_solve_triangular)/triangular_solve | solution.py:44
  185.6 1.7 convolution_subtract_fusion.2
  189.0 1.8 convolution_subtract_fusion.1
  195.3 10.4 %fusion = f32[1,1536,1536]{1,2,0:T(8,128)} fusion(f32[1536,1536]{0,1:T(8,128)S(1)} %bitcast_dynamic-update-slice_fusion.10, f32[128,1536]{1,0:T(8,128)S(1)} %fusion.66, f32[128,1536]{1,0:T(8,128)S(1)} %fusion.65, f32[1,1536,256]{1,2,0:T(8,128)S(1)} %constant_dynamic-update-slice_fusion.36), kind=kOutput, calls=%fused_computation.5 | convolution fusion | flops 7250509824 | bytes 22020096 | tf_op jit(solution)/shard_map/fik,fkj->fij/dot_general | solution.py:73
  205.8 4.1 collective-permute-start.1
  211.6 200.7 %collective-permute-done.1 = f32[1,1536,1536]{1,2,0:T(8,128)} collective-permute-done((f32[1,1536,1536]{1,2,0:T(8,128)}, f32[1,1536,1536]{1,2,0:T(8,128)}, u32[]{:S(2)}, u32[]{:S(2)}) %collective-permute-start.1) | collective-permute-done | bytes 9437216 | tf_op jit(solution)/shard_map/ppermute | solution.py:10
  412.2 7.5 %broadcast_select_fusion = (f32[1,1536,1536]{1,2,0:T(8,128)S(1)}, f32[1,1536,1536]{1,2,0:T(8,128)S(1)}) fusion(f32[1,1536,1536]{1,2,0:T(8,128)} %collective-permute-done.1, f32[1,1536,1536]{1,2,0:T(8,128)} %fusion, pred[]{:T(512)S(6)} %eq.8), kind=kLoop, calls=%fused_computation.6 | loop fusion | flops 4718592 | bytes 37748736 | tf_op jit(solution)/shard_map/jit(_where)/select_n | solution.py:91
  419.8 3.6 copy-done
  423.4 2.8 copy-done.1
  427.4 1.6 copy.25
  429.3 11.7 %custom-call.54 = f32[1,128,128]{2,1,0:T(8,128)S(1)} custom-call(f32[1,128,128]{2,1,0:T(8,128)S(1)} %cholesky.339), custom_call_target="Cholesky" | custom-call | tf_op jit(solution)/shard_map/jit(cholesky)/cholesky | solution.py:42
  441.2 1.9 slice_dynamic-update-slice_fusion.7
  443.0 2.3 constant_dynamic-update-slice_fusion.97
  445.3 2.2 constant_dynamic-update-slice_fusion.104
  448.9 9.8 %custom-call.55 = f32[1,1,128,128]{2,3,1,0:T(8,128)S(1)} custom-call(f32[1,1,128,128]{3,2,1,0:T(8,128)S(1)} %get-tuple-element.119), custom_call_target="InvertDiagBlocksLowerTriangular" | custom-call | tf_op jit(solution)/shard_map/jit(cholesky)/cholesky | solution.py:42
  459.4 11.7 %custom-call.56 = f32[1,128,128]{2,1,0:T(8,128)S(1)} custom-call(f32[1,128,128]{2,1,0:T(8,128)S(1)} %cholesky.343), custom_call_target="Cholesky" | custom-call | tf_op jit(solution)/shard_map/jit(cholesky)/cholesky | solution.py:42
  471.8 10.2 %custom-call.57 = f32[1,1,128,128]{2,3,1,0:T(8,128)S(1)} custom-call(f32[1,1,128,128]{3,2,1,0:T(8,128)S(1)} %get-tuple-element.116), custom_call_target="InvertDiagBlocksLowerTriangular" | custom-call | tf_op jit(solution)/shard_map/jit(cholesky)/cholesky | solution.py:42
  482.7 11.7 %custom-call.58 = f32[1,128,128]{2,1,0:T(8,128)S(1)} custom-call(f32[1,128,128]{2,1,0:T(8,128)S(1)} %cholesky.348), custom_call_target="Cholesky" | custom-call | tf_op jit(solution)/shard_map/jit(cholesky)/cholesky | solution.py:42
  495.1 9.8 %custom-call.63 = f32[1,1,128,128]{2,3,1,0:T(8,128)S(1)} custom-call(f32[1,1,128,128]{3,2,1,0:T(8,128)S(1)} %get-tuple-element.113), custom_call_target="InvertDiagBlocksLowerTriangular" | custom-call | tf_op jit(solution)/shard_map/jit(cholesky)/cholesky/custom-call.10 | solution.py:42
  505.5 11.8 %custom-call.59 = f32[1,128,128]{2,1,0:T(8,128)S(1)} custom-call(f32[1,128,128]{2,1,0:T(8,128)S(1)} %fusion.43), custom_call_target="Cholesky" | custom-call | tf_op jit(solution)/shard_map/jit(cholesky)/cholesky | solution.py:42
  520.8 7.8 %while.3 = (s32[]{:T(128)}, f32[512,512]{1,0:T(8,128)S(1)}, s32[4,2]{0,1:T(2,128)S(1)}, f32[4,128,128]{2,1,0:T(8,128)S(1)}, s32[]{:T(128)}) while((s32[]{:T(128)}, f32[512,512]{1,0:T(8,128)S(1)}, s32[4,2]{0,1:T(2,128)S(1)}, f32[4,128,128]{2,1,0:T(8,128)S(1)}, s32[]{:T(128)}) %tuple.97), condition=%wide.while_cond.1, body=%wide.while_body.1.sunk | while | flops 2 | bytes 131189 | solution.py:44
  528.6 39.3 %custom-call.60 = f32[4,128,128]{1,2,0:T(8,128)S(1)} custom-call(f32[4,128,128]{2,1,0:T(8,128)S(1)} %get-tuple-element.21), custom_call_target="InvertDiagBlocksLowerTriangular" | custom-call | tf_op jit(solution)/shard_map/jit(_solve_triangular)/triangular_solve | solution.py:44
  570.1 2.2 constant_dynamic-update-slice_fusion.102
  575.2 2.2 constant_dynamic-update-slice_fusion.100
  593.6 2.0 fusion.25
  602.4 2.1 fusion.22
  605.5 29.1 %fusion.1 = f32[2048,2048]{0,1:T(8,128)S(1)} fusion(f32[128,2048]{1,0:T(8,128)S(1)} %fusion.73, f32[128,2048]{1,0:T(8,128)S(1)} %fusion.71, f32[128,2048]{1,0:T(8,128)S(1)} %fusion.69, f32[128,2048]{1,0:T(8,128)S(1)} %fusion.68, f32[1,2048,512]{1,2,0:T(8,128)S(1)} %slice_dynamic-update-slice_fusion), kind=kOutput, calls=%fused_computation.9 | convolution fusion | flops 25772949504 | bytes 25165824 | tf_op jit(solution)/shard_map/fik,fkj->fij/dot_general | solution.py:73
  635.4 2.0 constant_dynamic-update-slice_fusion.95
  638.2 2.0 constant_dynamic-update-slice_fusion.93
  641.0 2.0 constant_dynamic-update-slice_fusion.91
  643.8 1.6 bitcast_dynamic-update-slice_fusion.9
  645.4 2.2 constant_dynamic-update-slice_fusion.98
  647.6 3.2 bitcast_dynamic-update-slice_fusion.8
  652.4 3.2 bitcast_dynamic-update-slice_fusion.6
  657.1 3.2 bitcast_dynamic-update-slice_fusion.4
  661.8 3.2 bitcast_dynamic-update-slice_fusion.2
  665.0 6.7 dynamic-slice_subtract_fusion
  671.7 5.3 copy.28
  (185 shorter events, 80.0 us)
Async XLA Ops:
  5.3 94.2 %collective-permute-start = (f32[1,1024,1024]{1,2,0:T(8,128)}, f32[1,1024,1024]{1,2,0:T(8,128)}, u32[]{:S(2)}, u32[]{:S(2)}) collective-permute-start(f32[1,1024,1024]{1,2,0:T(8,128)} %copy.16), channel_id=1, source_target_pairs={{0,2},{1,3},{2,0},{3,1},{4,6},{5,7},{6,4},{7,5},{8,10},{9,11},{10,... | collective-permute-start | bytes 12582920 | tf_op jit(solution)/shard_map/ppermute | solution.py:10
  104.0 2.0 copy-start.3
  106.1 1.2 copy-start.9
  107.3 1.1 copy-start.11
  108.4 1.2 copy-start.13
  109.6 1.2 copy-start.15
  110.8 1.1 copy-start.17
  113.8 0.8 copy-start.19
  188.1 3.4 copy-start.18
  188.9 2.6 copy-start.14
  189.0 2.7 copy-start.16
  191.5 1.4 copy-start.12
  193.2 1.4 copy-start.10
  205.8 206.5 %collective-permute-start.1 = (f32[1,1536,1536]{1,2,0:T(8,128)}, f32[1,1536,1536]{1,2,0:T(8,128)}, u32[]{:S(2)}, u32[]{:S(2)}) collective-permute-start(f32[1,1536,1536]{1,2,0:T(8,128)} %fusion), channel_id=1, source_target_pairs={{0,64},{4,68},{8,72},{12,76},{16,80},{20,84},{24,88},{28,92},{32,9... | collective-permute-start | bytes 28311560 | tf_op jit(solution)/shard_map/ppermute | solution.py:10
  419.8 3.6 copy-start
  419.8 6.4 copy-start.1
  427.4 1.7 copy-start.4
  572.3 8.0 %copy-start.2 = (f32[1,2048,512]{1,2,0:T(8,128)S(1)}, f32[1,2048,512]{1,2,0:T(8,128)}, u32[]{:S(2)}) copy-start(f32[1,2048,512]{1,2,0:T(8,128)} %slice_dynamic-update-slice_fusion.7) | copy-start | bytes 12582916
  605.5 29.9 %copy-start.7 = (f32[1,256,2048]{1,2,0:T(8,128)S(1)}, f32[1,256,2048]{1,2,0:T(8,128)}, u32[]{:S(2)}) copy-start(f32[1,256,2048]{1,2,0:T(8,128)} %get-tuple-element.81) | copy-start | bytes 6291460
  605.5 29.9 %copy-start.6 = (f32[1,256,2048]{1,2,0:T(8,128)S(1)}, f32[1,256,2048]{1,2,0:T(8,128)}, u32[]{:S(2)}) copy-start(f32[1,256,2048]{1,2,0:T(8,128)} %get-tuple-element.82) | copy-start | bytes 6291460
  605.5 29.9 %copy-start.5 = (f32[1,256,2048]{1,2,0:T(8,128)S(1)}, f32[1,256,2048]{1,2,0:T(8,128)}, u32[]{:S(2)}) copy-start(f32[1,256,2048]{1,2,0:T(8,128)} %get-tuple-element.83) | copy-start | bytes 6291460
  657.1 3.2 copy-start.8
where the time goes:
time: 688 us; the launch traced here: 677 us
  waiting for transfers between devices  291 us (42%)
  other arithmetic  197 us (29%)
  local copies, waits for them, and re-layouts  108 us (16%)
  matrix products  67.6 us (10%)
  starting transfers between devices  7.36 us (1%)
    ppermute x2, waiting for transfers between devices, partner_2(): return lax.ppermute(value, axis, pairs)  291 us
    another operation x22, other arithmetic, cholesky_apply(): factor = jnp.linalg.cholesky(coupling)  115 us
    unnamed x110, local copies, waits for them, and re-layouts  75.6 us
    another operation x6, other arithmetic, cholesky_apply(): jax.scipy.linalg.solve_triangular(factor, half_way, lower=True, trans=1)  60.7 us
    dot_general x2, matrix products, merge(): jnp.einsum('fik,fkj->fij', edge_rows, solved, precision=lax.Precision.HIG...  39.5 us
    another operation x23, local copies, waits for them, and re-layouts  20.4 us
  transfers between devices with their start and end apart: 2, of which 2 were waited for; matrix products, arithmetic and copies ran while one was open for 0% of the time, Pallas kernels for 0%

commit v1 on v0

v1 whole, which is shorter than its diff:
```python
import functools

import jax
import jax.numpy as jnp
from jax import lax
from jax.experimental import pallas as pl
from jax.experimental.pallas import tpu as pltpu
from jax.sharding import PartitionSpec as P

F32 = jnp.float32
BF16 = jnp.bfloat16
B = 128
W = 4


def solve_4(s, x):
    a0, a1, a2 = s[0, 0], s[1, 0], s[1, 1]
    b = [[s[2, 0], s[2, 1]], [s[3, 0], s[3, 1]]]
    r = 1.0 / (a0 * a2 - a1 * a1)
    e = [[b[i][0] * a2 - b[i][1] * a1, b[i][1] * a0 - b[i][0] * a1] for i in range(2)]
    f00 = e[0][0] * b[0][0] + e[0][1] * b[0][1]
    f10 = e[1][0] * b[0][0] + e[1][1] * b[0][1]
    f11 = e[1][0] * b[1][0] + e[1][1] * b[1][1]
    s0, s1, s2 = s[2, 2] - f00 * r, s[3, 2] - f10 * r, s[3, 3] - f11 * r
    q = 1.0 / (s0 * s2 - s1 * s1)
    t = [[e[i][j] * r for j in range(2)] for i in range(2)]
    y = [x[2 + i] - (t[i][0] * x[0] + t[i][1] * x[1]) for i in range(2)]
    w = [(a2 * x[0] - a1 * x[1]) * r, (a0 * x[1] - a1 * x[0]) * r]
    high = [(s2 * y[0] - s1 * y[1]) * q, (s0 * y[1] - s1 * y[0]) * q]
    low = [w[j] - (t[0][j] * high[0] + t[1][j] * high[1]) for j in range(2)]
    return low + high


def sweep(mats):
    lane_8 = lax.broadcasted_iota(jnp.int32, (8, B), 1)
    lane = lax.broadcasted_iota(jnp.int32, (B, B), 1)
    sub = lax.broadcasted_iota(jnp.int32, (B, B), 0)
    mats = list(mats)
    for k in range(0, B, W):
        inside_8 = (lane_8 >= k) & (lane_8 < k + W)
        below = (sub >= k) & (sub < k + W)
        inside = ((lane >= k) & (lane < k + W)) | below
        rows = [[jnp.broadcast_to(a[k + j : k + j + 1, :], (8, B)) for j in range(W)] for a in mats]
        s = [
            {
                (i, j): jnp.broadcast_to(row[j][:, k + i : k + i + 1], (8, B))
                for i in range(W)
                for j in range(i + 1)
            }
            for row in rows
        ]
        cols = [[jnp.broadcast_to(a[:, k + j : k + j + 1], (B, B)) for j in range(W)] for a in mats]
        for m in range(len(mats)):
            x = [
                jnp.where(inside_8, jnp.where(lane_8 == k + j, -1.0, 0.0), rows[m][j])
                for j in range(W)
            ]
            r = [jnp.concatenate([v] * (B // 8), axis=0) for v in solve_4(s[m], x)]
            base = jnp.where(inside, 0.0, mats[m])
            c = [
                jnp.where(below, jnp.where(sub == k + j, -1.0, 0.0), cols[m][j]) for j in range(W)
            ]
            mats[m] = base - ((c[0] * r[0] + c[1] * r[1]) + (c[2] * r[2] + c[3] * r[3]))
    return mats


def dot_full(a, b):
    return jnp.dot(a, b, precision=lax.Precision.HIGHEST, preferred_element_type=F32)


def block_sweep(refs, k):
    at = pl.ds(pl.multiple_of(k * B, B), B)
    swept = sweep([ref[at, at] for ref in refs])
    for ref, minus in zip(refs, swept):
        row = dot_full(-minus, ref[at, :])
        col = ref[:, at]
        ref[...] = ref[...] - dot_full(col, row)
        ref[at, :] = row
        ref[:, at] = dot_full(col, -minus)
        ref[at, at] = minus


def split(x):
    hi = x.astype(BF16)
    return hi, (x - hi.astype(F32)).astype(BF16)


def dot_split(a, b, transposed=False):
    dims = (((1,), (1 if transposed else 0,)), ((), ()))
    one = functools.partial(lax.dot_general, dimension_numbers=dims, preferred_element_type=F32)
    return one(a[0], b[0]) + (one(a[0], b[1]) + one(a[1], b[0]))


MESH = pl.DeviceIdType.MESH


def inverse_kernel(
    leaf,
    o,
    o_x,
    o_y,
    o_d,
    oo,
    oo_x,
    sides,
    u,
    s_inv,
    hh,
    hh_x,
    hh_sum,
    vv,
    hv,
    vv_y,
    hv_y,
    vv_sum,
    vv_x,
    hv_x,
    hv_d,
    local_sem,
    send_sem,
    recv_sem,
):
    e = hh.shape[0]
    nx, ny = lax.axis_size("gx"), lax.axis_size("gy")
    gx, gy = lax.axis_index("gx"), lax.axis_index("gy")
    across, above = lax.rem(gx + nx // 2, nx), lax.rem(gy + ny // 2, ny)
    cb, rb = gx // (nx // 2), gy // (ny // 2)
    mixed = cb != rb
    beside, over, corner = (across, gy), (gx, above), (across, above)

    def place(side):
        return pl.ds(pl.multiple_of(side * e, e), e)

    west, south, h, v = place(cb), place(2 + rb), place(1 - cb), place(3 - rb)

    def local(rows, cols, dst, index):
        return pltpu.make_async_copy(leaf.at[0, rows, cols], dst, local_sem.at[index])

    def send(src, dst, index, device):
        return pltpu.make_async_remote_copy(
            src_ref=src,
            dst_ref=dst,
            send_sem=send_sem.at[index],
            recv_sem=recv_sem.at[index],
            device_id=device,
            device_id_type=MESH,
        )

    first = [local(h, h, hh, 0), local(v, v, vv, 1), local(h, v, hv, 2)]
    rest = [
        local(west, h, o.at[:e, :e], 3),
        local(west, v, o.at[:e, e:], 4),
        local(south, h, o.at[e:, :e], 5),
        local(south, v, o.at[e:, e:], 6),
        local(west, west, oo.at[0], 7),
        local(west, south, oo.at[1], 8),
        local(south, south, oo.at[2], 9),
    ]
    for copy in first:
        copy.start()
    for copy in rest:
        copy.start()

    barrier = pltpu.get_barrier_semaphore()
    for device in (beside, over, corner):
        pl.semaphore_signal(barrier, inc=1, device_id=device, device_id_type=MESH)
    pl.semaphore_wait(barrier, 3)

    send_hh = send(hh, hh_x, 0, beside)
    send_vv = send(vv, vv_y, 1, over)
    send_hv_y = send(hv, hv_y, 2, over)
    send_hv = send(hv, hv_x, 3, beside)
    send_sum = send(hh_x, hh_sum, 4, over)
    send_vv_sum = send(vv_sum, vv_x, 5, beside)
    send_hv_d = send(hv_x, hv_d, 6, over)
    send_o_x = send(o, o_x, 7, beside)
    send_o_y = send(o, o_y, 8, over)
    send_o_d = send(o, o_d, 9, corner)
    send_oo = send(oo, oo_x, 10, beside)

    first[0].wait()
    send_hh.start()
    first[1].wait()
    send_vv.start()
    first[2].wait()
    send_hv_y.start()
    send_hh.wait_recv()
    hh_x[...] += hh[...]
    send_sum.start()
    send_hv.start()
    send_vv.wait_recv()
    vv_sum[...] = vv[...] + vv_y[...]
    send_vv_sum.start()
    for copy in rest:
        copy.wait()
    send_hv.wait_recv()
    send_hv_d.start()
    send_o_x.start()

    @pl.when(jnp.logical_not(mixed))
    def _():
        send_o_y.start()

    sides[0] = hh_x[...]
    send_sum.wait_recv()
    sides[1] = hh_sum[...]
    block_sweep([sides.at[0], sides.at[1]], 0)

    @pl.when(mixed)
    def _():
        send_o_d.start()
        send_oo.start()

    block_sweep([sides.at[0], sides.at[1]], 1)
    sides[...] = -sides[...]

    send_hv_y.wait_recv()
    send_hv_d.wait_recv()
    send_vv_sum.wait_recv()
    c = [
        jnp.concatenate([hv[...], hv_x[...]], axis=1),
        jnp.concatenate([hv_y[...], hv_d[...]], axis=1),
    ]
    for k in range(2):
        u[k] = dot_full(sides[k], c[k])
    both = jnp.concatenate(c, axis=0)
    s_inv[...] = -dot_full(both.T, jnp.concatenate([u[0], u[1]], axis=0))
    s_inv[:e, :e] += vv_sum[...]
    s_inv[e:, e:] += vv_x[...]

    @pl.loop(0, 2 * e // B)
    def _(k):
        block_sweep([s_inv], k)

    s_inv[...] = -s_inv[...]

    @pl.when(mixed)
    def _():
        send_o_y.wait_recv()
        send_o_d.wait()
        send_oo.wait_send()

    @pl.when(jnp.logical_not(mixed))
    def _():
        send_o_y.wait_send()
        send_oo.wait_recv()

    send_o_x.wait()
    for copy in (send_hh, send_vv, send_hv_y, send_hv, send_sum, send_vv_sum, send_hv_d):
        copy.wait_send()


def quarter_kernel(
    idx, o, o_x, o_y, o_d, oo, oo_x, sides, u, s_inv, out, pc_hi, pc_lo, s_hi, s_lo, h_hi, h_lo, u_hi, u_lo
):
    e = o.shape[0] // 2
    g = pl.program_id(0)
    x = idx[0]
    same = idx[4]
    r = g // 2

    def place(c):
        return x if c == 0 else 1 - x

    def fill(first, second, k):
        pair = split(u[k])
        for c, source in enumerate((first, second)):
            oh = source[:, :e]
            oh_pair = split(oh)
            value = -dot_split(oh_pair, pair)
            halves = [value[:, :e], value[:, e:]]
            halves[c] = halves[c] + source[:, e:]
            for part in range(2):
                start = pl.multiple_of((2 * part + place(c)) * e, e)
                rows = pl.ds(start, e)
                for q in range(2):
                    hi, lo = split(halves[q][part * e : (part + 1) * e, :])
                    pc_hi[rows, q * e : (q + 1) * e] = hi
                    pc_lo[rows, q * e : (q + 1) * e] = lo
                pc_hi[rows, 2 * e :] = oh_pair[0][part * e : (part + 1) * e, :]
                pc_lo[rows, 2 * e :] = oh_pair[1][part * e : (part + 1) * e, :]

    @pl.when(g == 0)
    def _():
        s_hi[...], s_lo[...] = split(s_inv[...])
        h_hi[...], h_lo[...] = split(sides[0])
        u_hi[...], u_lo[...] = split(u[0])

    @pl.when((g == 0) & (same == 1))
    def _():
        fill(o, o_x, 0)

    @pl.when((g == 0) & (same == 0))
    def _():
        fill(o_y, o_d, 1)

    part = pl.ds(pl.multiple_of((g % 2) * e, e), e)
    rows = jnp.where(r == 0, o[part, :], o_x[part, :])
    oh = split(rows[:, :e])
    ov = rows[:, e:]
    base = -dot_split(oh, (u_hi[...], u_lo[...]))
    left = base[:, :e] + jnp.where(r == 0, ov, 0.0)
    right = base[:, e:] + jnp.where(r == 0, 0.0, ov)
    p = split(jnp.concatenate([left, right], axis=1))
    gain = split(dot_split(p, (s_hi[...], s_lo[...])))

    @pl.when(same == 0)
    def _():
        out[...] = -dot_split(gain, (pc_hi[:, : 2 * e], pc_lo[:, : 2 * e]), True)

    @pl.when(same == 1)
    def _():
        side = split(dot_split(oh, (h_hi[...], h_lo[...])))
        both = tuple(jnp.concatenate([gain[k], side[k]], axis=1) for k in range(2))
        out[...] = -dot_split(both, (pc_hi[...], pc_lo[...]), True)
        where = jnp.where(r == 0, x, 1 - x)
        first = pl.ds(pl.multiple_of(where * e, e), e)
        second = pl.ds(pl.multiple_of((2 + where) * e, e), e)

        @pl.when(g % 2 == 0)
        def _():
            out[:, first] += jnp.where(r == 0, oo[0], oo_x[0])
            out[:, second] += jnp.where(r == 0, oo[1], oo_x[1])

        @pl.when(g % 2 == 1)
        def _():
            out[:, first] += jnp.where(r == 0, oo[1], oo_x[1]).T
            out[:, second] += jnp.where(r == 0, oo[2], oo_x[2])


def in_vmem(count):
    return [pl.BlockSpec(memory_space=pltpu.VMEM)] * count


def body(leaf_maps):
    size = leaf_maps.shape[1]
    e = size // 4
    column_bit = lax.axis_index("gx") // (lax.axis_size("gx") // 2)
    row_bit = lax.axis_index("gy") // (lax.axis_size("gy") // 2)
    same = column_bit == row_bit
    idx = jnp.stack(
        [column_bit, 2 + row_bit, 1 - column_bit, 3 - row_bit, same.astype(jnp.int32)]
    ).astype(jnp.int32)
    limit = 32 * 1024 * 1024
    half = (2 * e, 2 * e)
    block = pltpu.VMEM((e, e), F32)

    o, o_x, o_y, o_d, oo, oo_x, sides, u, s_inv = pl.pallas_call(
        inverse_kernel,
        in_specs=[pl.BlockSpec(memory_space=pltpu.HBM)],
        out_specs=in_vmem(9),
        out_shape=[jax.ShapeDtypeStruct(half, F32)] * 4
        + [jax.ShapeDtypeStruct((3, e, e), F32)] * 2
        + [
            jax.ShapeDtypeStruct((2, e, e), F32),
            jax.ShapeDtypeStruct((2, e, 2 * e), F32),
            jax.ShapeDtypeStruct(half, F32),
        ],
        scratch_shapes=[block] * 11
        + [
            pltpu.SemaphoreType.DMA((10,)),
            pltpu.SemaphoreType.DMA((11,)),
            pltpu.SemaphoreType.DMA((11,)),
        ],
        compiler_params=pltpu.CompilerParams(
            vmem_limit_bytes=limit, collective_id=0, has_side_effects=True
        ),
        cost_estimate=pl.CostEstimate(
            flops=4_000_000_000, bytes_accessed=12 * 2**20, transcendentals=0
        ),
        name="inverse",
    )(leaf_maps)

    def out_pick(g, s):
        r = g // 2
        return (0, 2 * (g % 2) + (1 - r) * s[0] + r * (1 - s[0]), 0)

    return pl.pallas_call(
        quarter_kernel,
        grid_spec=pltpu.PrefetchScalarGridSpec(
            num_scalar_prefetch=1,
            grid=(4,),
            in_specs=in_vmem(9),
            out_specs=pl.BlockSpec((None, e, size), out_pick),
            scratch_shapes=[
                pltpu.VMEM((size, 3 * e), BF16),
                pltpu.VMEM((size, 3 * e), BF16),
                pltpu.VMEM(half, BF16),
                pltpu.VMEM(half, BF16),
                pltpu.VMEM((e, e), BF16),
                pltpu.VMEM((e, e), BF16),
                pltpu.VMEM((e, 2 * e), BF16),
                pltpu.VMEM((e, 2 * e), BF16),
            ],
        ),
        out_shape=jax.ShapeDtypeStruct((1, size, size), F32),
        compiler_params=pltpu.CompilerParams(vmem_limit_bytes=limit),
        cost_estimate=pl.CostEstimate(flops=9_000_000_000, bytes_accessed=2**23, transcendentals=0),
        name="quarter",
    )(idx, o, o_x, o_y, o_d, oo, oo_x, sides, u, s_inv)


def solution(mesh):
    return jax.shard_map(
        body,
        mesh=mesh,
        in_specs=(P(None, "gy", "gx"),),
        out_specs=P(None, "gy", "gx"),
        check_vma=False,
    )
```

time: 688 us -> 101 us (0.15); the launches traced: 677 us -> 101 us
  waiting for transfers between devices: 291 us -> 0 us
  other arithmetic: 197 us -> 0 us
  local copies, waits for them, and re-layouts: 108 us -> 2.27 us
  Pallas kernels: 0 us -> 98.3 us
  matrix products: 67.6 us -> 0 us
  starting transfers between devices: 7.36 us -> 0 us
    ppermute x2 -> x0, waiting for transfers between devices: 291 us -> none  [partner_2(): return lax.ppermute(value, axis, pairs)]
    another operation x28 -> x0, other arithmetic: 176 us -> none  [the longest x22 115 us: cholesky_apply(): factor = jnp.linalg.cholesky(coupling)]
    pallas_call x0 -> x2, Pallas kernels: none -> 98.3 us  [the longest x1 84.8 us: body(): pl.pallas_call(inverse_kernel, in_specs=[pl.BlockSpec(memory_space=pltpu....]
    unnamed x110 -> x2, local copies, waits for them, and re-layouts: 75.6 us -> 2.19 us
    dot_general x2 -> x0, matrix products: 39.5 us -> none  [merge(): jnp.einsum('fik,fkj->fij', edge_rows, solved, precision=lax.Precision.HIG...]
    another operation x28 -> x0, matrix products: 28.1 us -> none  [the longest x10 12.1 us: cholesky_apply(): jax.scipy.linalg.solve_triangular(factor, half_way, lower=True, trans=1)]
    another operation x36 -> x1, local copies, waits for them, and re-layouts: 21.6 us -> 0.08 us  [body(): jnp.stack([column_bit, 2 + row_bit, 1 - column_bit, 3 - row_bit, same.ast...]
    select_n x2 -> x0, other arithmetic: 12 us -> none  [the longest x1 7.54 us: body(): right_map = jnp.where(column_bit == 0, beside, column_map)]
  transfers between devices with their start and end apart: 2 -> 0, of which waited for: 2 -> 0; matrix products, arithmetic and copies ran while one was open for 0% -> 0% of each run, Pallas kernels for 0% -> 0%
where the time goes in v1:
time: 101 us
  Pallas kernels  98.3 us (97%)
  local copies, waits for them, and re-layouts  2.27 us (2%)
    pallas_call x1, Pallas kernels, body(): pl.pallas_call(inverse_kernel, in_specs=[pl.BlockSpec(memory_space=pltpu....  84.8 us
    pallas_call x1, Pallas kernels, body(): pl.pallas_call(quarter_kernel, grid_spec=pltpu.PrefetchScalarGridSpec(num...  13.5 us
    unnamed x2, local copies, waits for them, and re-layouts  2.19 us

profile of v1, /device:TPU:0, one launch (start us, length us, event | category | flops | bytes accessed | tf_op | source)
XLA Modules:
  0.0 100.6 jit_solution(17538001366663844720)
XLA Ops:
  0.0 0.1 stack.27.idx
  0.1 0.0 copy-start
  0.1 2.2 %copy-done = f32[1,1024,1024]{2,1,0:T(8,128)S(1)} copy-done((f32[1,1024,1024]{2,1,0:T(8,128)S(1)}, f32[1,1024,1024]{2,1,0:T(8,128)}, u32[]{:S(2)}) %copy-start) | copy-done | bytes 4194328
  2.3 84.8 %inverse.1 = (f32[512,512]{1,0:T(8,128)S(1)}, f32[512,512]{1,0:T(8,128)S(1)}, f32[512,512]{1,0:T(8,128)S(1)}, f32[512,512]{1,0:T(8,128)S(1)}, f32[3,256,256]{2,1...) custom-call(f32[1,1024,1024]{2,1,0:T(8,128)S(1)} %copy-done), custom_call_target="tpu_custom_call" | custom-call | flops 4000000000 | bytes 12582912 | tf_op jit(solution)/shard_map/inverse/pallas_call | solution.py:348
  87.0 13.5 %quarter.1 = f32[1,1024,1024]{2,1,0:T(8,128)} custom-call(s32[5]{0:T(128)S(1)} %stack.27.idx, f32[512,512]{1,0:T(8,128)S(1)} %get-tuple-element.14.o, f32[512,512]{1,0:T(8,128)S(1)} %get-tuple-element.15.o_x, f32[512,512]{1,0:T(8,128)S(1)} %get-tuple-element.16.o_y, f32[512,512]{1,0:T(8,128)S(1)} %get-tuple-element.17.o_d, ...), custom_call_target="tpu_custom_call" | custom-call | flops 8999999488 | bytes 8388608 | tf_op jit(solution)/shard_map/quarter/pallas_call | solution.py:378
Async XLA Ops:
  0.1 2.2 %copy-start = (f32[1,1024,1024]{2,1,0:T(8,128)S(1)}, f32[1,1024,1024]{2,1,0:T(8,128)}, u32[]{:S(2)}) copy-start(f32[1,1024,1024]{2,1,0:T(8,128)} %leaf.1) | copy-start | bytes 12582916

commit v2 on v1

--- a/solution.py
+++ b/solution.py
@@ -64,25 +64,34 @@
     return mats
 
 
-def dot_full(a, b):
-    return jnp.dot(a, b, precision=lax.Precision.HIGHEST, preferred_element_type=F32)
+def split(x):
+    hi = x.astype(BF16)
+    return hi, (x - hi.astype(F32)).astype(BF16)
+
+
+def left_parts(pair):
+    return jnp.concatenate([pair[0], pair[0], pair[1]], axis=1)
+
+
+def right_parts(pair):
+    return jnp.concatenate([pair[0], pair[1], pair[0]], axis=0)
+
+
+def dot_parts(a, b):
+    return jnp.dot(a, b, preferred_element_type=F32)
 
 
 def block_sweep(refs, k):
     at = pl.ds(pl.multiple_of(k * B, B), B)
     swept = sweep([ref[at, at] for ref in refs])
     for ref, minus in zip(refs, swept):
-        row = dot_full(-minus, ref[at, :])
-        col = ref[:, at]
-        ref[...] = ref[...] - dot_full(col, row)
+        p = split(-minus)
+        col = left_parts(split(ref[:, at]))
+        row = dot_parts(left_parts(p), right_parts(split(ref[at, :])))
+        ref[...] = ref[...] - dot_parts(col, right_parts(split(row)))
         ref[at, :] = row
-        ref[:, at] = dot_full(col, -minus)
+        ref[:, at] = dot_parts(col, right_parts(p))
         ref[at, at] = minus
-
-
-def split(x):
-    hi = x.astype(BF16)
-    return hi, (x - hi.astype(F32)).astype(BF16)
 
 
 def dot_split(a, b, transposed=False):
@@ -107,7 +116,6 @@
     s_inv,
     hh,
     hh_x,
-    hh_sum,
     vv,
     hv,
     vv_y,
@@ -170,13 +178,14 @@
     send_vv = send(vv, vv_y, 1, over)
     send_hv_y = send(hv, hv_y, 2, over)
     send_hv = send(hv, hv_x, 3, beside)
-    send_sum = send(hh_x, hh_sum, 4, over)
+    send_side = send(sides.at[0], sides.at[1], 4, over)
     send_vv_sum = send(vv_sum, vv_x, 5, beside)
     send_hv_d = send(hv_x, hv_d, 6, over)
     send_o_x = send(o, o_x, 7, beside)
     send_o_y = send(o, o_y, 8, over)
-    send_o_d = send(o, o_d, 9, corner)
+    send_o_d = send(o.at[:e, :], o_d.at[:e, :], 9, corner)
     send_oo = send(oo, oo_x, 10, beside)
+    pass_o_d = send(o_x.at[e:, :], o_d.at[e:, :], 11, over)
 
     first[0].wait()
     send_hh.start()
@@ -185,68 +194,77 @@
     first[2].wait()
     send_hv_y.start()
     send_hh.wait_recv()
-    hh_x[...] += hh[...]
-    send_sum.start()
     send_hv.start()
+    sides[0] = hh[...] + hh_x[...]
+    block_sweep([sides.at[0]], 0)
     send_vv.wait_recv()
     vv_sum[...] = vv[...] + vv_y[...]
     send_vv_sum.start()
+    send_hv.wait_recv()
+    send_hv_d.start()
+    block_sweep([sides.at[0]], 1)
+    sides[0] = -sides[0]
+    send_side.start()
     for copy in rest:
         copy.wait()
-    send_hv.wait_recv()
-    send_hv_d.start()
     send_o_x.start()
 
-    @pl.when(jnp.logical_not(mixed))
-    def _():
-        send_o_y.start()
-
-    sides[0] = hh_x[...]
-    send_sum.wait_recv()
-    sides[1] = hh_sum[...]
-    block_sweep([sides.at[0], sides.at[1]], 0)
+    def couple(k, near, far):
+        c = jnp.concatenate([near[...], far[...]], axis=1)
+        c_pair = split(c)
+        value = dot_parts(left_parts(split(sides[k])), right_parts(c_pair))
+        u[k] = value
+        u_parts = right_parts(split(value))
+        c_parts = jnp.concatenate([c_pair[0].T, c_pair[0].T, c_pair[1].T], axis=1)
+        return dot_parts(c_parts, u_parts)
+
+    s_inv[...] = -couple(0, hv, hv_x)
+    send_hv_y.wait_recv()
+    send_vv_sum.wait_recv()
+    s_inv[:e, :e] += vv_sum[...]
+    s_inv[e:, e:] += vv_x[...]
+    send_hv_d.wait_recv()
+    send_side.wait_recv()
 
     @pl.when(mixed)
     def _():
         send_o_d.start()
         send_oo.start()
 
-    block_sweep([sides.at[0], sides.at[1]], 1)
-    sides[...] = -sides[...]
-
-    send_hv_y.wait_recv()
-    send_hv_d.wait_recv()
-    send_vv_sum.wait_recv()
-    c = [
-        jnp.concatenate([hv[...], hv_x[...]], axis=1),
-        jnp.concatenate([hv_y[...], hv_d[...]], axis=1),
-    ]
-    for k in range(2):
-        u[k] = dot_full(sides[k], c[k])
-    both = jnp.concatenate(c, axis=0)
-    s_inv[...] = -dot_full(both.T, jnp.concatenate([u[0], u[1]], axis=0))
-    s_inv[:e, :e] += vv_sum[...]
-    s_inv[e:, e:] += vv_x[...]
+    @pl.when(jnp.logical_not(mixed))
+    def _():
+        send_o_y.start()
+
+    s_inv[...] -= couple(1, hv_y, hv_d)
 
     @pl.loop(0, 2 * e // B)
     def _(k):
         block_sweep([s_inv], k)
 
+        @pl.when(k == e // B)
+        def _():
+            send_o_x.wait_recv()
+
+            @pl.when(jnp.logical_not(mixed))
+            def _():
+                pass_o_d.start()
+
     s_inv[...] = -s_inv[...]
 
     @pl.when(mixed)
     def _():
         send_o_y.wait_recv()
+        pass_o_d.wait_recv()
         send_o_d.wait()
         send_oo.wait_send()
 
     @pl.when(jnp.logical_not(mixed))
     def _():
         send_o_y.wait_send()
+        pass_o_d.wait_send()
         send_oo.wait_recv()
 
-    send_o_x.wait()
-    for copy in (send_hh, send_vv, send_hv_y, send_hv, send_sum, send_vv_sum, send_hv_d):
+    for copy in (send_hh, send_vv, send_hv_y, send_hv, send_side, send_vv_sum, send_hv_d, send_o_x):
         copy.wait_send()
 
 
@@ -356,11 +374,11 @@
             jax.ShapeDtypeStruct((2, e, 2 * e), F32),
             jax.ShapeDtypeStruct(half, F32),
         ],
-        scratch_shapes=[block] * 11
+        scratch_shapes=[block] * 10
         + [
             pltpu.SemaphoreType.DMA((10,)),
-            pltpu.SemaphoreType.DMA((11,)),
-            pltpu.SemaphoreType.DMA((11,)),
+            pltpu.SemaphoreType.DMA((12,)),
+            pltpu.SemaphoreType.DMA((12,)),
         ],
         compiler_params=pltpu.CompilerParams(
             vmem_limit_bytes=limit, collective_id=0, has_side_effects=True

time: 101 us -> 83.7 us (0.83)
  Pallas kernels: 98.3 us -> 81.2 us
    pallas_call x1, Pallas kernels: 84.8 us -> 67.9 us  [body(): pl.pallas_call(inverse_kernel, in_specs=[pl.BlockSpec(memory_space=pltpu....]
where the time goes in v2:
time: 83.7 us; the launch traced here: 83.5 us
  Pallas kernels  81.2 us (97%)
  local copies, waits for them, and re-layouts  2.27 us (3%)
    pallas_call x1, Pallas kernels, body(): pl.pallas_call(inverse_kernel, in_specs=[pl.BlockSpec(memory_space=pltpu....  67.9 us
    pallas_call x1, Pallas kernels, body(): pl.pallas_call(quarter_kernel, grid_spec=pltpu.PrefetchScalarGridSpec(num...  13.3 us
    unnamed x2, local copies, waits for them, and re-layouts  2.19 us

profile of v2, /device:TPU:0, one launch (start us, length us, event | category | flops | bytes accessed | tf_op | source)
XLA Modules:
  0.0 83.5 jit_solution(13775816277444092240)
XLA Ops:
  0.0 0.1 stack.27.idx
  0.1 0.0 copy-start
  0.1 2.2 %copy-done = f32[1,1024,1024]{2,1,0:T(8,128)S(1)} copy-done((f32[1,1024,1024]{2,1,0:T(8,128)S(1)}, f32[1,1024,1024]{2,1,0:T(8,128)}, u32[]{:S(2)}) %copy-start) | copy-done | bytes 4194328
  2.3 67.9 %inverse.1 = (f32[512,512]{1,0:T(8,128)S(1)}, f32[512,512]{1,0:T(8,128)S(1)}, f32[512,512]{1,0:T(8,128)S(1)}, f32[512,512]{1,0:T(8,128)S(1)}, f32[3,256,256]{2,1...) custom-call(f32[1,1024,1024]{2,1,0:T(8,128)S(1)} %copy-done), custom_call_target="tpu_custom_call" | custom-call | flops 4000000000 | bytes 12582912 | tf_op jit(solution)/shard_map/inverse/pallas_call | solution.py:366
  70.2 13.3 %quarter.1 = f32[1,1024,1024]{2,1,0:T(8,128)} custom-call(s32[5]{0:T(128)S(1)} %stack.27.idx, f32[512,512]{1,0:T(8,128)S(1)} %get-tuple-element.14.o, f32[512,512]{1,0:T(8,128)S(1)} %get-tuple-element.15.o_x, f32[512,512]{1,0:T(8,128)S(1)} %get-tuple-element.16.o_y, f32[512,512]{1,0:T(8,128)S(1)} %get-tuple-element.17.o_d, ...), custom_call_target="tpu_custom_call" | custom-call | flops 8999999488 | bytes 8388608 | tf_op jit(solution)/shard_map/quarter/pallas_call | solution.py:396
Async XLA Ops:
  0.1 2.2 %copy-start = (f32[1,1024,1024]{2,1,0:T(8,128)S(1)}, f32[1,1024,1024]{2,1,0:T(8,128)}, u32[]{:S(2)}) copy-start(f32[1,1024,1024]{2,1,0:T(8,128)} %leaf.1) | copy-start | bytes 12582916

commit v3 on v2

--- a/solution.py
+++ b/solution.py
@@ -1,5 +1,3 @@
-import functools
-
 import jax
 import jax.numpy as jnp
 from jax import lax
@@ -94,12 +92,6 @@
         ref[at, at] = minus
 
 
-def dot_split(a, b, transposed=False):
-    dims = (((1,), (1 if transposed else 0,)), ((), ()))
-    one = functools.partial(lax.dot_general, dimension_numbers=dims, preferred_element_type=F32)
-    return one(a[0], b[0]) + (one(a[0], b[1]) + one(a[1], b[0]))
-
-
 MESH = pl.DeviceIdType.MESH
 
 
@@ -113,6 +105,7 @@
     oo_x,
     sides,
     u,
+    lhs,
     s_inv,
     hh,
     hh_x,
@@ -241,7 +234,7 @@
     def _(k):
         block_sweep([s_inv], k)
 
-        @pl.when(k == e // B)
+        @pl.when(k == 2)
         def _():
             send_o_x.wait_recv()
 
@@ -249,7 +242,16 @@
             def _():
                 pass_o_d.start()
 
-    s_inv[...] = -s_inv[...]
+    s_parts = right_parts(split(s_inv[...]))
+    uh_parts = jnp.concatenate([right_parts(split(u[0])), right_parts(split(sides[0]))], axis=1)
+    for k, source in enumerate((o, o_x)):
+        both = dot_parts(left_parts(split(source[:, :e])), uh_parts)
+        halves = [-both[:, :e], -both[:, e : 2 * e]]
+        halves[k] = halves[k] + source[:, e:]
+        p = left_parts(split(jnp.concatenate(halves, axis=1)))
+        rows = slice(2 * k * e, 2 * (k + 1) * e)
+        lhs[rows, : 6 * e] = left_parts(split(dot_parts(p, s_parts)))
+        lhs[rows, 6 * e :] = left_parts(split(-both[:, 2 * e :]))
 
     @pl.when(mixed)
     def _():
@@ -268,9 +270,7 @@
         copy.wait_send()
 
 
-def quarter_kernel(
-    idx, o, o_x, o_y, o_d, oo, oo_x, sides, u, s_inv, out, pc_hi, pc_lo, s_hi, s_lo, h_hi, h_lo, u_hi, u_lo
-):
+def quarter_kernel(idx, o, o_x, o_y, o_d, oo, oo_x, u, lhs, out, pc):
     e = o.shape[0] // 2
     g = pl.program_id(0)
     x = idx[0]
@@ -280,57 +280,42 @@
     def place(c):
         return x if c == 0 else 1 - x
 
-    def fill(first, second, k):
-        pair = split(u[k])
+    def fill(first, second, u_parts):
         for c, source in enumerate((first, second)):
-            oh = source[:, :e]
-            oh_pair = split(oh)
-            value = -dot_split(oh_pair, pair)
+            pair = split(source[:, :e])
+            value = -dot_parts(left_parts(pair), u_parts)
             halves = [value[:, :e], value[:, e:]]
             halves[c] = halves[c] + source[:, e:]
             for part in range(2):
-                start = pl.multiple_of((2 * part + place(c)) * e, e)
-                rows = pl.ds(start, e)
+                rows = pl.ds(pl.multiple_of((2 * part + place(c)) * e, e), e)
+                of = slice(part * e, (part + 1) * e)
                 for q in range(2):
-                    hi, lo = split(halves[q][part * e : (part + 1) * e, :])
-                    pc_hi[rows, q * e : (q + 1) * e] = hi
-                    pc_lo[rows, q * e : (q + 1) * e] = lo
-                pc_hi[rows, 2 * e :] = oh_pair[0][part * e : (part + 1) * e, :]
-                pc_lo[rows, 2 * e :] = oh_pair[1][part * e : (part + 1) * e, :]
-
-    @pl.when(g == 0)
-    def _():
-        s_hi[...], s_lo[...] = split(s_inv[...])
-        h_hi[...], h_lo[...] = split(sides[0])
-        u_hi[...], u_lo[...] = split(u[0])
+                    hi, lo = split(halves[q][of, :])
+                    for n, piece in enumerate((hi, lo, hi)):
+                        pc[rows, (2 * n + q) * e : (2 * n + q + 1) * e] = piece
+                for n, piece in enumerate((pair[0], pair[1], pair[0])):
+                    pc[rows, (6 + n) * e : (7 + n) * e] = piece[of, :]
 
     @pl.when((g == 0) & (same == 1))
     def _():
-        fill(o, o_x, 0)
+        fill(o, o_x, right_parts(split(u[0])))
 
     @pl.when((g == 0) & (same == 0))
     def _():
-        fill(o_y, o_d, 1)
-
-    part = pl.ds(pl.multiple_of((g % 2) * e, e), e)
-    rows = jnp.where(r == 0, o[part, :], o_x[part, :])
-    oh = split(rows[:, :e])
-    ov = rows[:, e:]
-    base = -dot_split(oh, (u_hi[...], u_lo[...]))
-    left = base[:, :e] + jnp.where(r == 0, ov, 0.0)
-    right = base[:, e:] + jnp.where(r == 0, 0.0, ov)
-    p = split(jnp.concatenate([left, right], axis=1))
-    gain = split(dot_split(p, (s_hi[...], s_lo[...])))
+        fill(o_y, o_d, right_parts(split(u[1])))
+
+    rows = pl.ds(pl.multiple_of(g * e, e), e)
+
+    def times_columns(a, b):
+        return lax.dot_general(a, b, (((1,), (1,)), ((), ())), preferred_element_type=F32)
 
     @pl.when(same == 0)
     def _():
-        out[...] = -dot_split(gain, (pc_hi[:, : 2 * e], pc_lo[:, : 2 * e]), True)
+        out[...] = times_columns(lhs[rows, : 6 * e], pc[:, : 6 * e])
 
     @pl.when(same == 1)
     def _():
-        side = split(dot_split(oh, (h_hi[...], h_lo[...])))
-        both = tuple(jnp.concatenate([gain[k], side[k]], axis=1) for k in range(2))
-        out[...] = -dot_split(both, (pc_hi[...], pc_lo[...]), True)
+        out[...] = times_columns(lhs[rows, :], pc[...])
         where = jnp.where(r == 0, x, 1 - x)
         first = pl.ds(pl.multiple_of(where * e, e), e)
         second = pl.ds(pl.multiple_of((2 + where) * e, e), e)
@@ -363,7 +348,7 @@
     half = (2 * e, 2 * e)
     block = pltpu.VMEM((e, e), F32)
 
-    o, o_x, o_y, o_d, oo, oo_x, sides, u, s_inv = pl.pallas_call(
+    o, o_x, o_y, o_d, oo, oo_x, _, u, lhs = pl.pallas_call(
         inverse_kernel,
         in_specs=[pl.BlockSpec(memory_space=pltpu.HBM)],
         out_specs=in_vmem(9),
@@ -372,9 +357,10 @@
         + [
             jax.ShapeDtypeStruct((2, e, e), F32),
             jax.ShapeDtypeStruct((2, e, 2 * e), F32),
-            jax.ShapeDtypeStruct(half, F32),
+            jax.ShapeDtypeStruct((size, 9 * e), BF16),
         ],
-        scratch_shapes=[block] * 10
+        scratch_shapes=[pltpu.VMEM(half, F32)]
+        + [block] * 10
         + [
             pltpu.SemaphoreType.DMA((10,)),
             pltpu.SemaphoreType.DMA((12,)),
@@ -398,24 +384,17 @@
         grid_spec=pltpu.PrefetchScalarGridSpec(
             num_scalar_prefetch=1,
             grid=(4,),
-            in_specs=in_vmem(9),
+            in_specs=in_vmem(8),
             out_specs=pl.BlockSpec((None, e, size), out_pick),
             scratch_shapes=[
-                pltpu.VMEM((size, 3 * e), BF16),
-                pltpu.VMEM((size, 3 * e), BF16),
-                pltpu.VMEM(half, BF16),
-                pltpu.VMEM(half, BF16),
-                pltpu.VMEM((e, e), BF16),
-                pltpu.VMEM((e, e), BF16),
-                pltpu.VMEM((e, 2 * e), BF16),
-                pltpu.VMEM((e, 2 * e), BF16),
+                pltpu.VMEM((size, 9 * e), BF16),
             ],
         ),
         out_shape=jax.ShapeDtypeStruct((1, size, size), F32),
         compiler_params=pltpu.CompilerParams(vmem_limit_bytes=limit),
         cost_estimate=pl.CostEstimate(flops=9_000_000_000, bytes_accessed=2**23, transcendentals=0),
         name="quarter",
-    )(idx, o, o_x, o_y, o_d, oo, oo_x, sides, u, s_inv)
+    )(idx, o, o_x, o_y, o_d, oo, oo_x, u, lhs)
 
 
 def solution(mesh):

time: 83.7 us -> 80.5 us (0.962)
  Pallas kernels: 81.2 us -> 78 us
    pallas_call x1, Pallas kernels: 13.3 us -> 9.25 us  [body(): pl.pallas_call(quarter_kernel, grid_spec=pltpu.PrefetchScalarGridSpec(num...]
where the time goes in v3:
time: 80.5 us; the launch traced here: 80.2 us
  Pallas kernels  78 us (97%)
  local copies, waits for them, and re-layouts  2.27 us (3%)
    pallas_call x1, Pallas kernels, body(): pl.pallas_call(inverse_kernel, in_specs=[pl.BlockSpec(memory_space=pltpu....  68.7 us
    pallas_call x1, Pallas kernels, body(): pl.pallas_call(quarter_kernel, grid_spec=pltpu.PrefetchScalarGridSpec(num...  9.25 us
    unnamed x2, local copies, waits for them, and re-layouts  2.19 us

profile of v3, /device:TPU:0, one launch (start us, length us, event | category | flops | bytes accessed | tf_op | source)
XLA Modules:
  0.0 80.2 jit_solution(12538235418461979488)
XLA Ops:
  0.0 0.1 stack.27.idx
  0.1 0.0 copy-start
  0.1 2.2 %copy-done = f32[1,1024,1024]{2,1,0:T(8,128)S(1)} copy-done((f32[1,1024,1024]{2,1,0:T(8,128)S(1)}, f32[1,1024,1024]{2,1,0:T(8,128)}, u32[]{:S(2)}) %copy-start) | copy-done | bytes 4194328
  2.3 68.7 %inverse.1 = (f32[512,512]{1,0:T(8,128)S(1)}, f32[512,512]{1,0:T(8,128)S(1)}, f32[512,512]{1,0:T(8,128)S(1)}, f32[512,512]{1,0:T(8,128)S(1)}, f32[3,256,256]{2,1...) custom-call(f32[1,1024,1024]{2,1,0:T(8,128)S(1)} %copy-done), custom_call_target="tpu_custom_call" | custom-call | flops 4000000000 | bytes 12582912 | tf_op jit(solution)/shard_map/inverse/pallas_call | solution.py:351
  71.0 9.3 %quarter.1 = f32[1,1024,1024]{2,1,0:T(8,128)} custom-call(s32[5]{0:T(128)S(1)} %stack.27.idx, f32[512,512]{1,0:T(8,128)S(1)} %get-tuple-element.13.o, f32[512,512]{1,0:T(8,128)S(1)} %get-tuple-element.14.o_x, f32[512,512]{1,0:T(8,128)S(1)} %get-tuple-element.15.o_y, f32[512,512]{1,0:T(8,128)S(1)} %get-tuple-element.16.o_d, ...), custom_call_target="tpu_custom_call" | custom-call | flops 8999999488 | bytes 8388608 | tf_op jit(solution)/shard_map/quarter/pallas_call | solution.py:382
Async XLA Ops:
  0.1 2.2 %copy-start = (f32[1,1024,1024]{2,1,0:T(8,128)S(1)}, f32[1,1024,1024]{2,1,0:T(8,128)}, u32[]{:S(2)}) copy-start(f32[1,1024,1024]{2,1,0:T(8,128)} %leaf.1) | copy-start | bytes 12582916
